TPU v7x, 1024 devices: a whole 8x8x8 slice. The times are simulated.
1024 devices in a mesh: row: 32 (over x, y_hi), col: 32 (over z, y_lo, core).
Axes of the slice: x: 8, y: 8 (y_hi: 4, y_lo: 2; y = y_hi * 2 + y_lo), z: 8, core: 2. Of those that a mesh axis runs over, the one named last changes fastest.
Arguments:
- diag_inverse: bfloat16 [1376, 1376], P('row'), may hold values from -0.5 to 0.5, as said below
- row_u: bfloat16 [32, 1376, 224], P('row', None, 'col'), may hold values from -6 to 6
- row_v: bfloat16 [32, 1376, 224], P('row', None, 'col'), may hold values from -0.59765625 to 0.59765625
- col_u: bfloat16 [32, 1376, 224], P('col', None, 'row'), may hold values from -6 to 6
- col_v: bfloat16 [32, 1376, 224], P('col', None, 'row'), may hold values from -0.59765625 to 0.59765625
- tile_u: bfloat16 [32, 32, 1376, 224], P('row', 'col'), may hold values from -6 to 6
- tile_v: bfloat16 [32, 32, 1376, 224], P('row', 'col'), may hold values from -6 to 6
- sketch: bfloat16 [1376, 224], replicated, may hold values from -6 to 6
- row_rank: int32 [32], P('row'), may hold values from 56 to 224, as said below
- col_rank: int32 [32], P('col'), may hold values from 56 to 224, as said below
- old_rank: int32 [32, 32], P('row', 'col'), may hold values from 56 to 224, as said below
- new_rank: int32 [32, 32], P('row', 'col'), may hold values from 14 to 112, as said below
Outputs:
- new_u: bfloat16 [32, 32, 1376, 224], P('row', 'col')
- new_v: bfloat16 [32, 32, 1376, 224], P('row', 'col')
Inputs may be any that keep to these rules, and one draw needn't show every extreme that they name: diag_inverse is lower triangular with diagonal entries between 0.25 and 0.5. `row_rank`: some tile has rank 224. `col_rank`: some tile has rank 224. `old_rank`: some tile has rank 224. `new_rank`: each entry lies between old_rank // 4 and old_rank // 2 of the same tile; some tile has rank 224 // 2.
All inputs are finite; a program needn't handle non-finite values.
Results may differ from a plain program's by a relative error of at most 0.0085.
Values may be sent and summed in bfloat16 or wider, within the bound.
A program may use at most 64 MiB of HBM per device.

v0:
```python
import jax
import jax.numpy as jnp
from jax import lax
from jax.sharding import PartitionSpec as P

precise_mode = lax.Precision.HIGHEST


def gather_turned(arrays, axis, dims):
    turned = [jnp.moveaxis(a, dim, 0) for a, dim in zip(arrays, dims)]
    widths = [t[0].size for t in turned]
    both = jnp.concatenate([t.reshape(-1, w) for t, w in zip(turned, widths)], axis=1)
    result = lax.all_gather(both, axis, axis=0, tiled=True)
    tiles = jnp.split(result, [sum(widths[:k]) for k in range(1, len(widths))], axis=1)
    return tuple(
        (
            jnp.moveaxis(b.reshape(-1, *t.shape[1:]), 0, dim)
            for b, t, dim in zip(tiles, turned, dims)
        )
    )


def keep_mask(rank_cap, count):
    return jnp.arange(rank_cap, dtype=jnp.int32) < count


def solve_share(inverse, right_side, count):
    rank_cap = right_side.shape[2]
    keep_cols = jnp.arange(rank_cap, dtype=jnp.int32) < count
    values = jnp.where(keep_cols[None, :], right_side[0], jnp.zeros_like(right_side[0]))
    solved = jnp.dot(inverse, values, preferred_element_type=jnp.float32)
    return solved.astype(jnp.bfloat16)[None]


def tile_update(base_u, base_v, left_u, left_w, right_u, right_w, sketch, old_count, new_count):
    row_count, rank_cap = base_u.shape
    kept_v = jnp.where(keep_mask(rank_cap, old_count)[None, :], base_v, jnp.zeros_like(base_v))
    new_keep = keep_mask(rank_cap, new_count)
    probe_cols = jnp.where(new_keep[None, :], sketch, jnp.zeros_like(sketch))
    core_mat = jnp.dot(left_w.T, right_w, preferred_element_type=jnp.float32).astype(jnp.bfloat16)
    left_small = jnp.dot(kept_v.T, probe_cols, preferred_element_type=jnp.float32).astype(
        jnp.bfloat16
    )
    across = jnp.dot(right_u.T, probe_cols, preferred_element_type=jnp.float32).astype(jnp.bfloat16)
    middle = jnp.dot(core_mat, across, preferred_element_type=jnp.float32).astype(jnp.bfloat16)
    range_y = jnp.dot(base_u, left_small, preferred_element_type=jnp.float32) - jnp.dot(
        left_u, middle, preferred_element_type=jnp.float32
    )
    padding = jnp.where(new_keep, 0.0, 1.0).astype(jnp.float32)
    gram = jnp.dot(
        range_y.T, range_y, precision=precise_mode, preferred_element_type=jnp.float32
    ) + jnp.diag(padding)
    gram_factor = jnp.linalg.cholesky(gram)
    range_basis = jax.scipy.linalg.solve_triangular(gram_factor, range_y.T, lower=True).T
    new_u = (jnp.sqrt(jnp.float32(row_count)) * range_basis).astype(jnp.bfloat16)
    back_small = jnp.dot(base_u.T, new_u, preferred_element_type=jnp.float32).astype(jnp.bfloat16)
    side_small = jnp.dot(left_u.T, new_u, preferred_element_type=jnp.float32).astype(jnp.bfloat16)
    turned = jnp.dot(core_mat.T, side_small, preferred_element_type=jnp.float32).astype(
        jnp.bfloat16
    )
    summed = jnp.dot(kept_v, back_small, preferred_element_type=jnp.float32) - jnp.dot(
        right_u, turned, preferred_element_type=jnp.float32
    )
    new_v = (summed / jnp.float32(row_count)).astype(jnp.bfloat16)
    return (new_u, new_v)


def on_device(
    diag_inverse,
    row_u,
    row_v,
    col_u,
    col_v,
    tile_u,
    tile_v,
    sketch,
    row_rank,
    col_rank,
    old_rank,
    new_rank,
):
    inverse = lax.all_gather(diag_inverse, "row", axis=0, tiled=True)
    row_basis, row_right = gather_turned((row_u, row_v), "col", (2, 2))
    row_right = solve_share(inverse, row_right, row_rank[0])
    col_basis, col_right = (
        lax.all_gather(col_u, "row", axis=2, tiled=True),
        lax.all_gather(col_v, "row", axis=2, tiled=True),
    )
    col_right = solve_share(inverse, col_right, col_rank[0])
    new_u, new_v = tile_update(
        tile_u[0, 0],
        tile_v[0, 0],
        row_basis[0],
        row_right[0],
        col_basis[0],
        col_right[0],
        sketch,
        old_rank[0, 0],
        new_rank[0, 0],
    )
    return (new_u[None, None], new_v[None, None])


def solution(mesh):
    in_specs = (
        P("row", None),
        P("row", None, "col"),
        P("row", None, "col"),
        P("col", None, "row"),
        P("col", None, "row"),
        P("row", "col", None, None),
        P("row", "col", None, None),
        P(),
        P("row"),
        P("col"),
        P("row", "col"),
        P("row", "col"),
    )
    out_specs = (P("row", "col", None, None), P("row", "col", None, None))
    return jax.shard_map(
        on_device, mesh=mesh, in_specs=in_specs, out_specs=out_specs, check_vma=False
    )
```

profile of v0, /device:TPU:14, one launch (start us, length us, event | category | flops | bytes accessed | tf_op | source)
XLA Modules:
  0.0 314.3 jit_solution(18050722809121027860)
XLA Ops:
  7.2 1.5 maximum_bitcast_fusion
  8.9 0.7 all-gather.7.cloned.1.call-update
  9.6 0.8 copy.25
  12.9 0.8 copy.26
  13.8 95.0 %all_gather.15 = bf16[1,1376,224]{1,0,2:T(2,128)(2,1)} all-gather(bf16[1,1376,7]{1,0,2:T(2,128)(2,1)S(1)} %copy.26), channel_id=1, replica_groups=mesh['row'=32,'col'=32] {'row'}, dimensions={2}, use_global_device_ids=true | all-gather | bytes 635712 | tf_op jit(solution)/shard_map/all_gather | solution.py:86
  108.8 1.7 convolution_convert_fusion.2
  110.5 107.6 %all_gather.14 = bf16[1,1376,224]{1,0,2:T(2,128)(2,1)S(1)} all-gather(bf16[1,1376,7]{1,0,2:T(2,128)(2,1)S(1)} %copy.25), channel_id=1, replica_groups=mesh['row'=32,'col'=32] {'row'}, dimensions={2}, use_global_device_ids=true | all-gather | bytes 635712 | tf_op jit(solution)/shard_map/all_gather | solution.py:87
  218.0 1.8 reshape.94
  219.9 6.0 %reshape.96 = bf16[1376,1376]{1,0:T(8,128)(2,1)} reshape(bf16[32,43,1376]{2,1,0:T(8,128)(2,1)} %all-gather.7.cloned.1.call-done) | data formatting | bytes 7573504
  225.9 4.4 %convolution_convert_fusion = bf16[224,1376]{1,0:T(8,128)(2,1)} fusion(bf16[1376,1376]{1,0:T(8,128)(2,1)} %reshape.96, bf16[1,1376,224]{1,0,2:T(2,128)(2,1)S(1)} %all_gather.14, pred[224]{0:T(512)(128)(4,1)S(1)} %iota_compare_fusion.8), kind=kOutput, calls=%fused_computation.4 | convolution fusion | flops 848848896 | bytes 5019872 | tf_op jit(solution)/shard_map/dot_general | solution.py:31
  230.3 4.0 %convolution_convert_fusion.3 = bf16[224,224]{1,0:T(8,128)(2,1)S(1)} fusion(bf16[224,1376]{1,0:T(8,128)(2,1)} %convolution_convert_fusion, bf16[1376,1376]{1,0:T(8,128)(2,1)} %reshape.96, bf16[224,2752]{1,0:T(8,128)(2,1)S(1)} %reshape.94, pred[224]{0:T(512)(128)(4,1)S(1)} %iota_compare_fusion.9), kind=kOutput, calls=%fused_computation.14 | convolution fusion | flops 986983424 | bytes 5134848 | tf_op jit(solution)/shard_map/dot_general | solution.py:40
  234.3 0.6 fusion.5
  235.0 3.5 %bitcast_subtract_fusion = (f32[224,1376]{1,0:T(8,128)S(1)}, f32[224,1376]{1,0:T(8,128)}) fusion(f32[1376,224]{0,1:T(8,128)S(1)} %fusion.5, bf16[1,1,1376,224]{2,3,1,0:T(8,128)(2,1)S(1)} %copy-done, bf16[1376,224]{0,1:T(8,128)(2,1)} %param.19, pred[224]{0:T(512)(128)(4,1)S(1)} %get-tuple-element.38, bf16[1,1,1376,224]{2,3,1,0:T(8,128)(2,1)} %param.18, ...), kind=kOutput, calls=%fused_computation.10 | convolution fusion | flops 277143552 | bytes 5548480 | tf_op jit(solution)/shard_map/dot_general | solution.py:46
  238.4 3.1 fusion.4
  241.5 0.1 copy.27
  241.8 11.7 %cholesky.50 = f32[128,128]{1,0:T(8,128)S(1)} custom-call(f32[128,128]{1,0:T(8,128)S(1)} %cholesky.121), custom_call_target="Cholesky" | custom-call | tf_op jit(solution)/shard_map/jit(cholesky)/cholesky | solution.py:53
  253.6 9.8 %custom-call.15 = f32[1,128,128]{1,2,0:T(8,128)S(1)} custom-call(f32[1,128,128]{2,1,0:T(8,128)S(1)} %get-tuple-element.31), custom_call_target="InvertDiagBlocksLowerTriangular" | custom-call | tf_op jit(solution)/shard_map/jit(cholesky)/cholesky | solution.py:53
  263.4 0.2 constant_dynamic-update-slice_fusion.1
  263.6 0.2 convolution_subtract_fusion.2
  263.8 8.9 %cholesky.108 = f32[96,96]{1,0:T(8,128)S(1)} custom-call(f32[96,96]{1,0:T(8,128)S(1)} %convolution_subtract_fusion.2), custom_call_target="Cholesky" | custom-call | tf_op jit(solution)/shard_map/jit(cholesky)/cholesky | solution.py:53
  272.7 0.6 compare_reduce_fusion.1
  273.4 0.6 compare_reduce_fusion
  275.4 19.7 %custom-call.16 = f32[2,128,128]{1,2,0:T(8,128)S(1)} custom-call(f32[2,128,128]{2,1,0:T(8,128)S(1)} %pad_maximum_fusion), custom_call_target="InvertDiagBlocksLowerTriangular" | custom-call | tf_op jit(solution)/shard_map/jit(_solve_triangular)/triangular_solve | solution.py:54
  295.1 1.3 fusion.7
  296.4 0.8 convolution_subtract_fusion.1
  297.3 1.3 fusion.32
  298.6 1.1 fusion.45
  299.7 0.4 copy-done.2
  300.1 0.6 convolution_convert_fusion.7
  300.7 2.2 copy.29
  302.9 1.7 convolution_bitcast_fusion
  304.5 2.9 fusion.2
  (32 shorter events, 0.5 us)
Async XLA Ops:
  7.2 227.8 %copy-start = (bf16[1,1,1376,224]{2,3,1,0:T(8,128)(2,1)S(1)}, bf16[1,1,1376,224]{2,3,1,0:T(8,128)(2,1)}, u32[]{:S(2)}) copy-start(bf16[1,1,1376,224]{2,3,1,0:T(8,128)(2,1)} %param.17) | copy-start | bytes 1849348
  7.2 101.6 %copy-start.3 = (bf16[1376,224]{0,1:T(8,128)(2,1)S(1)}, bf16[1376,224]{0,1:T(8,128)(2,1)}, u32[]{:S(2)}) copy-start(bf16[1376,224]{0,1:T(8,128)(2,1)} %param.19) | copy-start | bytes 1849348
  7.2 210.8 %all-gather.5.cloned.1.call-start = ((), (), s32[]{:S(2)}) async-start(), calls=%async_computation | async-start | bytes 1486848 | tf_op jit(solution)/shard_map/all_gather | solution.py:13
  8.8 211.1 %all-gather.7.cloned.1.call-start = ((), (), s32[]{:S(2)}) async-start(), calls=%async_computation.1 | async-start | bytes 4460544 | tf_op jit(solution)/shard_map/all_gather | solution.py:82
  219.9 14.4 %copy-start.1 = (bf16[224,2752]{1,0:T(8,128)(2,1)}, bf16[224,2752]{1,0:T(8,128)(2,1)S(1)}, u32[]{:S(2)}) copy-start(bf16[224,2752]{1,0:T(8,128)(2,1)S(1)} %reshape.94) | copy-start | bytes 3698692
  234.3 4.1 %copy-start.4 = (bf16[224,224]{1,0:T(8,128)(2,1)}, bf16[224,224]{1,0:T(8,128)(2,1)S(1)}, u32[]{:S(2)}) copy-start(bf16[224,224]{1,0:T(8,128)(2,1)S(1)} %convolution_convert_fusion.3) | copy-start | bytes 301060
  298.6 1.6 copy-start.2
  298.6 1.5 copy-start.5
Sparse Core Ops, SparseCore 0:
  11.3 81.9 all-gather.4
  97.6 113.5 all-gather.6
where the time goes:
time: 315 us; the launch traced here: 314 us
  blocking collectives  203 us (64%)
  other arithmetic  54.4 us (17%)
  matrix products  26.2 us (8%)
  between operations  18.2 us (6%)
  local copies, waits for them, and re-layouts  12.2 us (4%)
    all_gather x1, blocking collectives, on_device(): lax.all_gather(col_v, 'row', axis=2, tiled=True)  108 us
    all_gather x1, blocking collectives, on_device(): lax.all_gather(col_u, 'row', axis=2, tiled=True)  95 us
    another operation x7, other arithmetic, tile_update(): gram_factor = jnp.linalg.cholesky(gram)  31.8 us
    another operation x6, other arithmetic, tile_update(): jax.scipy.linalg.solve_triangular(gram_factor, range_y.T, lower=True)  19.8 us
    unnamed x17, local copies, waits for them, and re-layouts  12.1 us
  transfers between devices with their start and end apart: 2, of which 0 were waited for; matrix products, arithmetic and copies ran while one was open for 2% of the time, Pallas kernels for 0%

commit v1 on v0

v1 whole, which is shorter than its diff:
```python
import jax
import jax.numpy as jnp
from jax import lax
from jax.experimental import pallas as pl
from jax.experimental.pallas import tpu as pltpu
from jax.sharding import PartitionSpec as P

NB = 1376
RANK = 224
HALF = 128
ROWS = 48
PANELS = 14
LANES = (384, 768, 1152, 1376)
HIGH = lax.Precision.HIGHEST
MESH_ID = pl.DeviceIdType.MESH
VMEM_LIMIT = 56 * 1024 * 1024


def dot_nt(a, b, **kw):
    return lax.dot_general(a, b, (((1,), (1,)), ((), ())), preferred_element_type=jnp.float32, **kw)


def dot_nn(a, b, **kw):
    return lax.dot_general(a, b, (((1,), (0,)), ((), ())), preferred_element_type=jnp.float32, **kw)


def prepare_kernel(row_rank, col_rank, diag, ru, rv, cu, cv, rs, cs, ds):
    col = lax.axis_index("col")
    row = lax.axis_index("row")
    zero_row = jnp.zeros((1, NB), jnp.bfloat16)
    spot = lax.broadcasted_iota(jnp.int32, (7, NB), 0)
    for u, v, out, first, count in ((ru, rv, rs, 7 * col, row_rank[0]), (cu, cv, cs, 7 * row, col_rank[0])):
        out[0, 0:7, :] = u[...]
        out[0, 7:8, :] = zero_row
        kept = jnp.where(spot + first < count, v[...].astype(jnp.float32), 0.0)
        out[1, 0:7, :] = kept.astype(jnp.bfloat16)
        out[1, 7:8, :] = zero_row
    ds[0:43, :] = diag[...]
    ds[43:48, :] = jnp.zeros((5, NB), jnp.bfloat16)


def prepare(row_rank, col_rank, diag, ru, rv, cu, cv):
    vmem = pl.BlockSpec(memory_space=pltpu.VMEM)
    return pl.pallas_call(
        prepare_kernel,
        name="prepare",
        in_specs=[pl.BlockSpec(memory_space=pltpu.SMEM)] * 2 + [vmem] * 5,
        out_specs=[vmem] * 3,
        out_shape=[
            jax.ShapeDtypeStruct((2, 8, NB), jnp.bfloat16),
            jax.ShapeDtypeStruct((2, 8, NB), jnp.bfloat16),
            jax.ShapeDtypeStruct((ROWS, NB), jnp.bfloat16),
        ],
    )(row_rank, col_rank, diag, ru, rv, cu, cv)


def gather_kernel(rs, cs, ds, r_all, c_all, d_all, own, quad_s, quad_r, zs, zr, ys, yr, xs, xr,
                  dys, dyr, dxs, dxr, ps, pr):
    row, col = lax.axis_index("row"), lax.axis_index("col")
    x, yh = row // 4, row % 4
    z, q = col // 4, col % 4
    core = col % 2

    def mate(k):
        low = jnp.where(k % 2 == 1, 1 - q % 2, q % 2)
        high = jnp.where(k // 2 == 1, 1 - q // 2, q // 2)
        return (row, z * 4 + high * 2 + low)

    def along_z(step):
        return (row, ((z + step) % 8) * 4 + q)

    def along_y(step):
        return (x * 4 + (yh + step) % 4, col)

    def along_x(step):
        return (((x + step) % 8) * 4 + yh, col)

    def remote(src, send, recv, device):
        return pltpu.make_async_remote_copy(
            src_ref=src, dst_ref=src, send_sem=send, recv_sem=recv, device_id=device, device_id_type=MESH_ID
        )

    partners = (
        [mate(1), mate(2), mate(3), along_z(1), along_z(7)]
        + [along_y(1), along_y(2), along_y(3), along_x(1), along_x(7)]
    )
    barrier = pltpu.get_barrier_semaphore()
    for device in partners:
        pl.semaphore_signal(barrier, inc=1, device_id=device, device_id_type=MESH_ID)
    local = [
        pltpu.make_async_copy(cs, c_all.at[x, yh], own.at[0]),
        pltpu.make_async_copy(ds, d_all.at[x, yh], own.at[1]),
        pltpu.make_async_copy(rs, r_all.at[z, q], own.at[2]),
    ]
    for copy in local:
        copy.start()
    pl.semaphore_wait(barrier, len(partners))
    for copy in local:
        copy.wait()

    sent = []

    def go(copy):
        copy.start()
        sent.append(copy.wait_send)

    for t in (1, 2, 3):
        go(remote(c_all.at[x, yh], ys.at[t], yr.at[t], along_y(t)))

    @pl.when(yh // 2 == core)
    def _():
        for t in (1, 2, 3):
            remote(d_all.at[x, yh], dys.at[t], dyr.at[yh % 2], along_y(t)).start()

    def sent_d():
        @pl.when(yh // 2 == core)
        def _():
            for t in (1, 2, 3):
                remote(d_all.at[x, yh], dys.at[t], dyr.at[yh % 2], along_y(t)).wait_send()

    sent.append(sent_d)
    for k in (1, 2, 3):
        go(remote(r_all.at[z, q], quad_s.at[k], quad_r.at[k], mate(k)))

    def by_class(xo, act):
        for k, lanes in enumerate(LANES):
            @pl.when(xo // 2 == k)
            def _(lanes=lanes):
                act(lanes)

    def ring_length(way, part, parts):
        return 4 if (part < parts // 2) == (way == 0) else 3

    def z_copy(way, step, k):
        zo = (z + (8 - step if way == 0 else step)) % 8
        slot = mate(k)[1] % 4
        return remote(r_all.at[zo, slot], zs.at[way, step, k], zr.at[way, step, k], along_z(1 if way == 0 else 7))

    def x_copy(way, step, t):
        xo = (x + (8 - step if way == 0 else step)) % 8
        return remote(
            c_all.at[xo, (yh + 4 - t) % 4], xs.at[way, step, t], xr.at[way, step, t], along_x(1 if way == 0 else 7)
        )

    def dx_do(way, step, b, method):
        xo = (x + (8 - step if way == 0 else step)) % 8

        def act(lanes):
            copy = remote(
                d_all.at[xo, 2 * core + b, :, pl.ds(0, lanes)],
                dxs.at[way, step, b], dxr.at[way, step, b], along_x(1 if way == 0 else 7),
            )
            getattr(copy, method)()

        by_class(xo, act)

    def share_do(way, step, b, method):
        xo = (x + (8 - step if way == 0 else step)) % 8
        theirs = method == "wait_recv"
        block = 2 * (1 - core if theirs else core) + b
        index = step if way == 0 else 4 + step

        def act(lanes):
            copy = remote(d_all.at[xo, block, :, pl.ds(0, lanes)], ps.at[index, b], pr.at[index, b], mate(1))
            getattr(copy, method)()

        if step == 0:
            @pl.when(block != yh)
            def _():
                by_class(xo, act)
        else:
            by_class(xo, act)

    def arrive_z(way, step, k):
        zo = (z + (8 - step if way == 0 else step)) % 8
        slot = mate(k)[1] % 4
        remote(r_all.at[zo, slot], zs.at[way, step - 1, k], zr.at[way, step - 1, k], along_z(1)).wait_recv()

    def arrive_x(way, step, t):
        xo = (x + (8 - step if way == 0 else step)) % 8
        remote(
            c_all.at[xo, (yh + 4 - t) % 4], xs.at[way, step - 1, t], xr.at[way, step - 1, t], along_x(1)
        ).wait_recv()

    def arrive_dx(way, step, b):
        xo = (x + (8 - step if way == 0 else step)) % 8

        def act(lanes):
            remote(
                d_all.at[xo, 2 * core + b, :, pl.ds(0, lanes)],
                dxs.at[way, step - 1, b], dxr.at[way, step - 1, b], along_x(1),
            ).wait_recv()

        by_class(xo, act)

    for step in range(5):
        for k in range(4):
            if step == 0 and k > 0:
                remote(r_all.at[z, mate(k)[1] % 4], quad_s.at[k], quad_r.at[k], mate(k)).wait_recv()
            for way in (0, 1):
                length = ring_length(way, k, 4)
                if 1 <= step <= length:
                    arrive_z(way, step, k)
                if step < length:
                    go(z_copy(way, step, k))
        for t in range(4):
            if step == 0 and t > 0:
                remote(c_all.at[x, (yh + 4 - t) % 4], ys.at[t], yr.at[t], along_y(t)).wait_recv()
            for way in (0, 1):
                length = ring_length(way, t, 4)
                if 1 <= step <= length:
                    arrive_x(way, step, t)
                if step < length:
                    go(x_copy(way, step, t))
            if t % 2 == 0:
                continue
            b = t // 2
            if step == 0:
                @pl.when(2 * core + b != yh)
                def _(b=b):
                    remote(d_all.at[x, 2 * core + b], dys.at[1], dyr.at[b], along_y(1)).wait_recv()
            for way in (0, 1):
                length = ring_length(way, b, 2)
                if 1 <= step <= length:
                    arrive_dx(way, step, b)
                if step < length:
                    dx_do(way, step, b, "start")
                    sent.append(lambda way=way, step=step, b=b: dx_do(way, step, b, "wait_send"))
                if (step == 0 and way == 0) or 1 <= step <= length:
                    share_do(way, step, b, "start")
                    sent.append(lambda way=way, step=step, b=b: share_do(way, step, b, "wait_send"))
    for b in (0, 1):
        for way in (0, 1):
            for step in range(ring_length(way, b, 2) + 1):
                if step > 0 or way == 0:
                    share_do(way, step, b, "wait_recv")
    for wait in sent:
        wait()


def gather(rs, cs, ds):
    dma = pltpu.SemaphoreType.DMA
    anywhere = pl.BlockSpec(memory_space=pl.ANY)
    return pl.pallas_call(
        gather_kernel,
        name="gather",
        in_specs=[anywhere] * 3,
        out_specs=[anywhere] * 3,
        out_shape=[
            jax.ShapeDtypeStruct((8, 4, 2, 8, NB), jnp.bfloat16),
            jax.ShapeDtypeStruct((8, 4, 2, 8, NB), jnp.bfloat16),
            jax.ShapeDtypeStruct((8, 4, ROWS, NB), jnp.bfloat16),
        ],
        scratch_shapes=[
            dma((3,)), dma((4,)), dma((4,)), dma((2, 4, 4)), dma((2, 4, 4)), dma((4,)), dma((4,)),
            dma((2, 4, 4)), dma((2, 4, 4)), dma((4,)), dma((2,)), dma((2, 4, 2)), dma((2, 4, 2)),
            dma((9, 2)), dma((9, 2)),
        ],
        compiler_params=pltpu.CompilerParams(collective_id=0, has_side_effects=True),
    )(rs, cs, ds)


def inverse_factor(gram):
    a = [gram[8 * i : 8 * i + 8, :] for i in range(PANELS)]
    lane = lax.broadcasted_iota(jnp.int32, (8, HALF), 1)
    line = lax.broadcasted_iota(jnp.int32, (8, HALF), 0)
    w = [jnp.where(lane == line + 8 * i, 1.0, 0.0).astype(jnp.float32) for i in range(PANELS)]
    done = []
    for k in range(PANELS):
        at = 8 * k
        d = [[jnp.broadcast_to(a[k][i : i + 1, at + j : at + j + 1], (8, HALF)) for j in range(i + 1)] for i in range(8)]
        low = [[None] * 8 for _ in range(8)]
        inv = []
        for j in range(8):
            inv.append(lax.rsqrt(d[j][j]))
            for i in range(j + 1, 8):
                low[i][j] = d[i][j] * inv[j]
            for i in range(j + 1, 8):
                for m in range(j + 1, i + 1):
                    d[i][m] = d[i][m] - low[i][j] * low[m][j]
        rows_a = [jnp.broadcast_to(a[k][i : i + 1, :], (8, HALF)) for i in range(8)]
        rows_w = [jnp.broadcast_to(w[k][i : i + 1, :], (8, HALF)) for i in range(8)]
        for j in range(8):
            rows_a[j] = rows_a[j] * inv[j]
            rows_w[j] = rows_w[j] * inv[j]
            for i in range(j + 1, 8):
                rows_a[i] = rows_a[i] - low[i][j] * rows_a[j]
                rows_w[i] = rows_w[i] - low[i][j] * rows_w[j]
        for i in range(k + 1, PANELS):
            cols = [jnp.broadcast_to(a[i][:, at + j : at + j + 1], (8, HALF)) for j in range(8)]
            for j in range(8):
                cols[j] = cols[j] * inv[j]
                for m in range(j + 1, 8):
                    cols[m] = cols[m] - cols[j] * low[m][j]
                a[i] = a[i] - cols[j] * rows_a[j]
                w[i] = w[i] - cols[j] * rows_w[j]
        final = rows_w[0]
        for j in range(1, 8):
            final = jnp.where(line == j, rows_w[j], final)
        done.append(final)
    done.append(jnp.zeros((HALF - 8 * PANELS, HALF), jnp.float32))
    return jnp.concatenate(done, axis=0)


def update_kernel(old_rank, new_rank, r_all, c_all, d_all, tu, tv, sk, new_u, new_v, solved, range_y):
    bf = jnp.bfloat16
    f32 = jnp.float32
    old_count, new_count = old_rank[0, 0], new_rank[0, 0]
    ru = r_all[:, 0].reshape(256, NB)
    rv = r_all[:, 1].reshape(256, NB)
    cu = c_all[:, 0].reshape(256, NB)
    cv = c_all[:, 1].reshape(256, NB)
    new_line = lax.broadcasted_iota(jnp.int32, (HALF, NB), 0)
    probe = jnp.where(new_line < new_count, sk[0:HALF, :].astype(f32), 0.0).astype(bf)
    old_keep = lax.broadcasted_iota(jnp.int32, (HALF, RANK), 1) < old_count
    left_small = jnp.where(old_keep, dot_nt(probe, tv[...]), 0.0).astype(bf)
    across = dot_nt(probe, cu).astype(bf)
    base = dot_nn(left_small, tu[...])
    vs = jnp.concatenate([rv, cv], axis=0)
    for xo in range(8):
        lanes = LANES[xo // 2]
        block = d_all[xo, :, :, 0:lanes].reshape(4 * ROWS, lanes)
        solved[:, pl.ds(4 * ROWS * xo, 4 * ROWS)] = dot_nt(vs[:, 0:lanes], block).astype(bf)
    core = dot_nt(solved[0:256, :], solved[256:512, :]).astype(bf)
    middle = dot_nt(across, core).astype(bf)
    y = base - dot_nn(middle, ru)
    range_y[...] = y
    gram = dot_nt(y, y, precision=HIGH)
    lane = lax.broadcasted_iota(jnp.int32, (HALF, HALF), 1)
    line = lax.broadcasted_iota(jnp.int32, (HALF, HALF), 0)
    gram = gram + jnp.where((lane == line) & (line >= new_count), 1.0, 0.0)
    inverse = inverse_factor(gram)
    u = (jnp.sqrt(f32(NB)) * dot_nn(inverse, range_y[...], precision=HIGH)).astype(bf)
    new_u[0:HALF, :] = u
    new_u[HALF:RANK, :] = jnp.zeros((RANK - HALF, NB), bf)
    back = jnp.where(old_keep, dot_nt(u, tu[...]), 0.0).astype(bf)
    side = dot_nt(u, ru).astype(bf)
    turned = dot_nn(side, core).astype(bf)
    new_v[0:HALF, :] = ((dot_nn(back, tv[...]) - dot_nn(turned, cu)) / f32(NB)).astype(bf)
    new_v[HALF:RANK, :] = jnp.zeros((RANK - HALF, NB), bf)


def update(old_rank, new_rank, r_all, c_all, d_all, tu, tv, sk):
    vmem = pl.BlockSpec(memory_space=pltpu.VMEM)
    out = jax.ShapeDtypeStruct((RANK, NB), jnp.bfloat16)
    return pl.pallas_call(
        update_kernel,
        name="update",
        in_specs=[pl.BlockSpec(memory_space=pltpu.SMEM)] * 2 + [vmem] * 6,
        out_specs=[vmem] * 2,
        out_shape=[out, out],
        scratch_shapes=[pltpu.VMEM((512, 32 * ROWS), jnp.bfloat16), pltpu.VMEM((HALF, NB), jnp.float32)],
        compiler_params=pltpu.CompilerParams(vmem_limit_bytes=VMEM_LIMIT),
    )(old_rank, new_rank, r_all.reshape(32, 2, 8, NB), c_all.reshape(32, 2, 8, NB), d_all, tu, tv, sk)


def on_device(diag_inverse, row_u, row_v, col_u, col_v, tile_u, tile_v, sketch, row_rank, col_rank, old_rank, new_rank):
    rs, cs, ds = prepare(row_rank, col_rank, diag_inverse, row_u[0].T, row_v[0].T, col_u[0].T, col_v[0].T)
    r_all, c_all, d_all = gather(rs, cs, ds)
    new_u, new_v = update(old_rank, new_rank, r_all, c_all, d_all, tile_u[0, 0].T, tile_v[0, 0].T, sketch.T)
    return (new_u.T[None, None], new_v.T[None, None])


def solution(mesh):
    in_specs = (
        P("row", None),
        P("row", None, "col"),
        P("row", None, "col"),
        P("col", None, "row"),
        P("col", None, "row"),
        P("row", "col", None, None),
        P("row", "col", None, None),
        P(),
        P("row"),
        P("col"),
        P("row", "col"),
        P("row", "col"),
    )
    out_specs = (P("row", "col", None, None), P("row", "col", None, None))
    return jax.shard_map(
        on_device, mesh=mesh, in_specs=in_specs, out_specs=out_specs, check_vma=False
    )
```

time: 315 us -> 92.7 us (0.29)
  the two profiles are of different devices: /device:TPU:14 before, /device:TPU:39 now
where the time goes in v1:
time: 92.7 us; the launch traced here: 92.5 us
  Pallas kernels  89.3 us (96%)
  between operations  3.22 us (3%)
    pallas_call x1, Pallas kernels, gather(): pl.pallas_call(gather_kernel, name='gather', in_specs=[anywhere] * 3, out...  72.7 us
    pallas_call x1, Pallas kernels, update(): pl.pallas_call(update_kernel, name='update', in_specs=[pl.BlockSpec(memor...  14.9 us

profile of v1, /device:TPU:39, one launch (start us, length us, event | category | flops | bytes accessed | tf_op | source)
XLA Modules:
  0.0 92.5 jit_solution(16138494548449862832)
XLA Ops:
  3.2 1.7 %prepare.1 = (bf16[2,8,1376]{2,1,0:T(8,128)(2,1)}, bf16[2,8,1376]{2,1,0:T(8,128)(2,1)}, bf16[48,1376]{1,0:T(8,128)(2,1)}) custom-call(s32[1]{0:T(128)S(6)} %copy.14.row_rank, s32[1]{0:T(128)S(6)} %copy.15.col_rank, bf16[43,1376]{1,0:T(8,128)(2,1)} %diag.1, bf16[7,1376]{1,0:T(8,128)(2,1)} %bitcast.32, bf16[7,1376]{1,0:T(8,128)(2,1)} %bitcast.33, ...), custom_call_target="tpu_custom_call" | custom-call | tf_op jit(solution)/shard_map/prepare/pallas_call | solution.py:44
  4.9 72.7 %gather.1 = (bf16[8,4,2,8,1376]{4,3,2,1,0:T(8,128)(2,1)}, bf16[8,4,2,8,1376]{4,3,2,1,0:T(8,128)(2,1)}, bf16[8,4,48,1376]{3,2,1,0:T(8,128)(2,1)}) custom-call(bf16[2,8,1376]{2,1,0:T(8,128)(2,1)} %get-tuple-element.10.rs, bf16[2,8,1376]{2,1,0:T(8,128)(2,1)} %get-tuple-element.11.cs, bf16[48,1376]{1,0:T(8,128)(2,1)} %get-tuple-element.12.ds), custom_call_target="tpu_custom_call" | custom-call | tf_op jit(solution)/shard_map/gather/pallas_call | solution.py:244
  77.6 14.9 %update.1 = (bf16[224,1376]{1,0:T(8,128)(2,1)}, bf16[224,1376]{1,0:T(8,128)(2,1)}) custom-call(s32[1,1]{1,0:T(1,128)S(6)} %copy.16.old_rank, s32[1,1]{1,0:T(1,128)S(6)} %copy.17.new_rank, bf16[32,2,8,1376]{3,2,1,0:T(8,128)(2,1)} %bitcast.27, bf16[32,2,8,1376]{3,2,1,0:T(8,128)(2,1)} %bitcast.28, bf16[8,4,48,1376]{3,2,1,0:T(8,128)(2,1)} %get-tuple-element.15.d_all, ...), custom_call_target="tpu_custom_call" | custom-call | tf_op jit(solution)/shard_map/update/pallas_call | solution.py:346

commit v2 on v1

--- a/solution.py
+++ b/solution.py
@@ -54,35 +54,42 @@
     )(row_rank, col_rank, diag, ru, rv, cu, cv)
 
 
-def gather_kernel(rs, cs, ds, r_all, c_all, d_all, own, quad_s, quad_r, zs, zr, ys, yr, xs, xr,
-                  dys, dyr, dxs, dxr, ps, pr):
+def gather_kernel(rs, cs, ds, r_all, c_all, d_all, own, quad_s, quad_r, zs, zr, zps, zpr, ys, yr, xs, xr,
+                  dxs, dxr, dfs, dfr, dhs, dhr, dbs, ps, pr):
     row, col = lax.axis_index("row"), lax.axis_index("col")
     x, yh = row // 4, row % 4
     z, q = col // 4, col % 4
-    core = col % 2
+    low, core = q // 2, q % 2
+
+    def quad(k):
+        there = jnp.where(k % 2 == 1, 1 - core, core)
+        return jnp.where(k // 2 == 1, 1 - low, low) * 2 + there
 
     def mate(k):
-        low = jnp.where(k % 2 == 1, 1 - q % 2, q % 2)
-        high = jnp.where(k // 2 == 1, 1 - q // 2, q // 2)
-        return (row, z * 4 + high * 2 + low)
+        return (row, z * 4 + quad(k))
 
     def along_z(step):
-        return (row, ((z + step) % 8) * 4 + q)
+        return (row, (z + step) % 8 * 4 + q)
 
     def along_y(step):
         return (x * 4 + (yh + step) % 4, col)
 
     def along_x(step):
-        return (((x + step) % 8) * 4 + yh, col)
-
-    def remote(src, send, recv, device):
+        return ((x + step) % 8 * 4 + yh, col)
+
+    def beside(way):
+        there = yh + low if way == 0 else yh + low + 3
+        return (x * 4 + there % 4, z * 4 + (1 - low) * 2 + core)
+
+    def remote(src, dst, send, recv, device):
         return pltpu.make_async_remote_copy(
-            src_ref=src, dst_ref=src, send_sem=send, recv_sem=recv, device_id=device, device_id_type=MESH_ID
+            src_ref=src, dst_ref=dst, send_sem=send, recv_sem=recv, device_id=device, device_id_type=MESH_ID
         )
 
+    across_pair = (x * 4 + (yh + 2 * low + 3) % 4, z * 4 + (1 - low) * 2 + core)
     partners = (
-        [mate(1), mate(2), mate(3), along_z(1), along_z(7)]
-        + [along_y(1), along_y(2), along_y(3), along_x(1), along_x(7)]
+        [mate(1), mate(2), mate(3), along_z(1), along_z(7), across_pair]
+        + [along_y(1), along_y(2), along_y(3), along_x(1), along_x(2), along_x(6), along_x(7)]
     )
     barrier = pltpu.get_barrier_semaphore()
     for device in partners:
@@ -95,32 +102,12 @@
     for copy in local:
         copy.start()
     pl.semaphore_wait(barrier, len(partners))
-    for copy in local:
-        copy.wait()
-
-    sent = []
+
+    ends = []
 
     def go(copy):
         copy.start()
-        sent.append(copy.wait_send)
-
-    for t in (1, 2, 3):
-        go(remote(c_all.at[x, yh], ys.at[t], yr.at[t], along_y(t)))
-
-    @pl.when(yh // 2 == core)
-    def _():
-        for t in (1, 2, 3):
-            remote(d_all.at[x, yh], dys.at[t], dyr.at[yh % 2], along_y(t)).start()
-
-    def sent_d():
-        @pl.when(yh // 2 == core)
-        def _():
-            for t in (1, 2, 3):
-                remote(d_all.at[x, yh], dys.at[t], dyr.at[yh % 2], along_y(t)).wait_send()
-
-    sent.append(sent_d)
-    for k in (1, 2, 3):
-        go(remote(r_all.at[z, q], quad_s.at[k], quad_r.at[k], mate(k)))
+        ends.append(copy.wait_send)
 
     def by_class(xo, act):
         for k, lanes in enumerate(LANES):
@@ -128,114 +115,188 @@
             def _(lanes=lanes):
                 act(lanes)
 
-    def ring_length(way, part, parts):
-        return 4 if (part < parts // 2) == (way == 0) else 3
+    def origin(here, way, step):
+        return (here + (8 - step if way == 0 else step)) % 8
+
+    def z_length(way, k):
+        return 4 if (k == 0) == (way == 0) else 3
 
     def z_copy(way, step, k):
-        zo = (z + (8 - step if way == 0 else step)) % 8
-        slot = mate(k)[1] % 4
-        return remote(r_all.at[zo, slot], zs.at[way, step, k], zr.at[way, step, k], along_z(1 if way == 0 else 7))
-
-    def x_copy(way, step, t):
-        xo = (x + (8 - step if way == 0 else step)) % 8
-        return remote(
-            c_all.at[xo, (yh + 4 - t) % 4], xs.at[way, step, t], xr.at[way, step, t], along_x(1 if way == 0 else 7)
+        slot = r_all.at[origin(z, way, step), quad(k)]
+        src = rs if step == 0 and k == 0 else slot
+        return remote(src, slot, zs.at[way, step, k // 2], zr.at[way, step, k // 2], along_z(1 if way == 0 else 7))
+
+    def z_tick(step):
+        for k in (0, 2):
+            if step == 0 and k == 2:
+                remote(rs, r_all.at[z, quad(2)], quad_s.at[2], quad_r.at[2], mate(2)).wait_recv()
+            for way in (0, 1):
+                if 1 <= step <= z_length(way, k):
+                    slot = r_all.at[origin(z, way, step), quad(k)]
+                    remote(slot, slot, zs.at[way, step - 1, k // 2], zr.at[way, step - 1, k // 2], mate(1)).wait_recv()
+                if step < z_length(way, k):
+                    go(z_copy(way, step, k))
+                if 1 <= step <= z_length(way, k):
+                    sems = (zps.at[way, step - 1, k // 2], zpr.at[way, step - 1, k // 2])
+                    go(remote(slot, slot, *sems, mate(1)))
+                    theirs = r_all.at[origin(z, way, step), quad(k + 1)]
+                    ends.append(remote(theirs, theirs, *sems, mate(1)).wait_recv)
+
+    def x_length(way, t):
+        return 4 if (t % 2 == 1) == (way == 0) else 3
+
+    def x_tick(t, step):
+        if step == 0 and t > 0:
+            remote(cs, c_all.at[x, (yh + 4 - t) % 4], ys.at[t], yr.at[t], along_y(t)).wait_recv()
+        for way in (0, 1):
+            slot = c_all.at[origin(x, way, step), (yh + 4 - t) % 4]
+            ahead = along_x(1 if way == 0 else 7)
+            if 1 <= step <= x_length(way, t):
+                remote(slot, slot, xs.at[way, step - 1, t], xr.at[way, step - 1, t], ahead).wait_recv()
+            if step < x_length(way, t):
+                src = cs if step == 0 and t == 0 else slot
+                go(remote(src, slot, xs.at[way, step, t], xr.at[way, step, t], ahead))
+
+    chunks = [(0, 0), (0, 1), (1, 1), (0, 2), (1, 2), (0, 3), (1, 3), (0, 4)]
+
+    def d_part(xo, there, half, lanes):
+        return d_all.at[xo, there % 4, half, :, pl.ds(0, lanes)]
+
+    def d_run(method, j, there, send, recv, device, mine=False):
+        xo = origin(x, *chunks[j])
+
+        def act(lanes):
+            part = d_part(xo, there, core, lanes)
+            src = ds.at[core, :, pl.ds(0, lanes)] if mine else part
+            getattr(remote(src, part, send, recv, device), method)()
+
+        by_class(xo, act)
+
+    def d_send(*args, when=None, **kw):
+        if when is None:
+            d_run("start", *args, **kw)
+            ends.append(lambda: d_run("wait_send", *args, **kw))
+        else:
+            guarded(low == when, lambda: d_run("start", *args, **kw))
+            ends.append(lambda: guarded(low == when, lambda: d_run("wait_send", *args, **kw)))
+
+    def d_wait(j, there, half, send, recv):
+        xo = origin(x, *chunks[j])
+
+        def act(lanes):
+            part = d_part(xo, there, half, lanes)
+            remote(part, part, send, recv, mate(1)).wait_recv()
+
+        by_class(xo, act)
+
+    def share(j, there, index):
+        sems = (ps.at[index, j], pr.at[index, j])
+        d_send(j, there, *sems, mate(1))
+        ends.append(lambda: d_wait(j, there, 1 - core, *sems))
+
+    def guarded(condition, act):
+        @pl.when(condition)
+        def _():
+            act()
+
+    def y_send(way, j, full, when):
+        base = yh + low + 3 if way == 0 else yh + low
+        if full:
+            mine = j == 0 and when == 1 - way
+            d_send(j, base, dfs.at[way, j], dfr.at[way, j], beside(way), when=when, mine=mine)
+        else:
+            there = base + 3 if way == 0 else base + 1
+            beyond = along_y(1 if way == 0 else 3)
+            d_send(j, there, dbs.at[way, j], dhr.at[way, j], beyond, when=when)
+            d_send(j, there, dhs.at[way, j], dhr.at[way, j], beside(way), when=when)
+
+    def late_share(j, there, index, when):
+        sems = (ps.at[index, j], pr.at[index, j])
+        d_send(j, there, *sems, mate(1), when=when)
+        ends.append(lambda: guarded(low == when, lambda: d_wait(j, there, 1 - core, *sems)))
+
+    reached = [0, 1, 1, 1, 1, 2, 2, 2]
+
+    def y_tick(tick):
+        order = sorted(range(8), key=lambda j: reached[j])
+        for hop in (0, 1, 2, 3):
+            for j in order:
+                if tick - reached[j] != hop:
+                    continue
+                for way in (0, 1):
+                    first = 1 - way
+                    half = j % 2 == way
+                    beside_pair = yh + 3 if way == 0 else yh + 1
+                    if hop == 0:
+                        y_send(way, j, True, first)
+                    elif hop in (1, 2):
+                        here = 1 - first if hop == 1 else first
+                        guarded(
+                            low == here,
+                            lambda: d_wait(j, beside_pair, core, dfs.at[way, j], dfr.at[way, j]),
+                        )
+                        if hop == 1:
+                            y_send(way, j, True, here)
+                        elif half:
+                            y_send(way, j, False, here)
+                        late_share(j, beside_pair, 1 + way, here)
+                    elif half:
+                        d_wait(j, yh + 2, core, dhs.at[way, j], dhr.at[way, j])
+                        share(j, yh + 2, 3)
+
+    def dx_send(way, far, step, mine):
+        j = 0 if mine else chunks.index((way, 2))
+        d_send(
+            j, yh, dxs.at[way, far - 1], dxr.at[way, far - 1], along_x(step if way == 0 else 8 - step), mine=mine
         )
 
-    def dx_do(way, step, b, method):
-        xo = (x + (8 - step if way == 0 else step)) % 8
-
-        def act(lanes):
-            copy = remote(
-                d_all.at[xo, 2 * core + b, :, pl.ds(0, lanes)],
-                dxs.at[way, step, b], dxr.at[way, step, b], along_x(1 if way == 0 else 7),
-            )
-            getattr(copy, method)()
-
-        by_class(xo, act)
-
-    def share_do(way, step, b, method):
-        xo = (x + (8 - step if way == 0 else step)) % 8
-        theirs = method == "wait_recv"
-        block = 2 * (1 - core if theirs else core) + b
-        index = step if way == 0 else 4 + step
-
-        def act(lanes):
-            copy = remote(d_all.at[xo, block, :, pl.ds(0, lanes)], ps.at[index, b], pr.at[index, b], mate(1))
-            getattr(copy, method)()
-
-        if step == 0:
-            @pl.when(block != yh)
-            def _():
-                by_class(xo, act)
-        else:
-            by_class(xo, act)
-
-    def arrive_z(way, step, k):
-        zo = (z + (8 - step if way == 0 else step)) % 8
-        slot = mate(k)[1] % 4
-        remote(r_all.at[zo, slot], zs.at[way, step - 1, k], zr.at[way, step - 1, k], along_z(1)).wait_recv()
-
-    def arrive_x(way, step, t):
-        xo = (x + (8 - step if way == 0 else step)) % 8
-        remote(
-            c_all.at[xo, (yh + 4 - t) % 4], xs.at[way, step - 1, t], xr.at[way, step - 1, t], along_x(1)
-        ).wait_recv()
-
-    def arrive_dx(way, step, b):
-        xo = (x + (8 - step if way == 0 else step)) % 8
-
-        def act(lanes):
-            remote(
-                d_all.at[xo, 2 * core + b, :, pl.ds(0, lanes)],
-                dxs.at[way, step - 1, b], dxr.at[way, step - 1, b], along_x(1),
-            ).wait_recv()
-
-        by_class(xo, act)
-
-    for step in range(5):
-        for k in range(4):
-            if step == 0 and k > 0:
-                remote(r_all.at[z, mate(k)[1] % 4], quad_s.at[k], quad_r.at[k], mate(k)).wait_recv()
+    def dx_wait(way, far):
+        d_wait(chunks.index((way, far)), yh, core, dxs.at[way, far - 1], dxr.at[way, far - 1])
+
+    def dx_tick(tick):
+        if tick == 0:
             for way in (0, 1):
-                length = ring_length(way, k, 4)
-                if 1 <= step <= length:
-                    arrive_z(way, step, k)
-                if step < length:
-                    go(z_copy(way, step, k))
-        for t in range(4):
-            if step == 0 and t > 0:
-                remote(c_all.at[x, (yh + 4 - t) % 4], ys.at[t], yr.at[t], along_y(t)).wait_recv()
+                dx_send(way, 2, 2, True)
             for way in (0, 1):
-                length = ring_length(way, t, 4)
-                if 1 <= step <= length:
-                    arrive_x(way, step, t)
-                if step < length:
-                    go(x_copy(way, step, t))
-            if t % 2 == 0:
-                continue
-            b = t // 2
-            if step == 0:
-                @pl.when(2 * core + b != yh)
-                def _(b=b):
-                    remote(d_all.at[x, 2 * core + b], dys.at[1], dyr.at[b], along_y(1)).wait_recv()
+                dx_send(way, 1, 1, True)
+        if tick == 1:
+            dx_wait(0, 2)
+            dx_send(0, 4, 2, False)
+            dx_send(0, 3, 1, False)
+            dx_wait(1, 2)
+            dx_send(1, 3, 1, False)
             for way in (0, 1):
-                length = ring_length(way, b, 2)
-                if 1 <= step <= length:
-                    arrive_dx(way, step, b)
-                if step < length:
-                    dx_do(way, step, b, "start")
-                    sent.append(lambda way=way, step=step, b=b: dx_do(way, step, b, "wait_send"))
-                if (step == 0 and way == 0) or 1 <= step <= length:
-                    share_do(way, step, b, "start")
-                    sent.append(lambda way=way, step=step, b=b: share_do(way, step, b, "wait_send"))
-    for b in (0, 1):
-        for way in (0, 1):
-            for step in range(ring_length(way, b, 2) + 1):
-                if step > 0 or way == 0:
-                    share_do(way, step, b, "wait_recv")
-    for wait in sent:
+                dx_wait(way, 1)
+        if tick == 2:
+            for way in (0, 1):
+                dx_wait(way, 3)
+            dx_wait(0, 4)
+        for j in range(1, 8):
+            if reached[j] == tick:
+                share(j, yh, 0)
+
+    for t in (1, 2, 3):
+        go(remote(cs, c_all.at[x, yh], ys.at[t], yr.at[t], along_y(t)))
+    for k in (2, 1, 3):
+        copy = remote(rs, r_all.at[z, q], quad_s.at[k], quad_r.at[k], mate(k))
+        go(copy)
+        if k != 2:
+            theirs = r_all.at[z, quad(k)]
+            ends.append(remote(theirs, theirs, quad_s.at[k], quad_r.at[k], mate(k)).wait_recv)
+    for tick in range(6):
+        if tick <= 2:
+            dx_tick(tick)
+        y_tick(tick)
+        if tick <= 4:
+            x_tick(0, tick)
+            z_tick(tick)
+        if tick >= 1:
+            for t in (1, 3, 2):
+                x_tick(t, tick - 1)
+    for wait in ends:
         wait()
+    for copy in local:
+        copy.wait()
 
 
 def gather(rs, cs, ds):
@@ -249,12 +310,12 @@
         out_shape=[
             jax.ShapeDtypeStruct((8, 4, 2, 8, NB), jnp.bfloat16),
             jax.ShapeDtypeStruct((8, 4, 2, 8, NB), jnp.bfloat16),
-            jax.ShapeDtypeStruct((8, 4, ROWS, NB), jnp.bfloat16),
+            jax.ShapeDtypeStruct((8, 4, 2, ROWS // 2, NB), jnp.bfloat16),
         ],
         scratch_shapes=[
-            dma((3,)), dma((4,)), dma((4,)), dma((2, 4, 4)), dma((2, 4, 4)), dma((4,)), dma((4,)),
-            dma((2, 4, 4)), dma((2, 4, 4)), dma((4,)), dma((2,)), dma((2, 4, 2)), dma((2, 4, 2)),
-            dma((9, 2)), dma((9, 2)),
+            dma((3,)), dma((4,)), dma((4,)), dma((2, 4, 2)), dma((2, 4, 2)), dma((2, 4, 2)), dma((2, 4, 2)),
+            dma((4,)), dma((4,)), dma((2, 4, 4)), dma((2, 4, 4)), dma((2, 4)), dma((2, 4)),
+            dma((2, 8)), dma((2, 8)), dma((2, 8)), dma((2, 8)), dma((2, 8)), dma((4, 8)), dma((4, 8)),
         ],
         compiler_params=pltpu.CompilerParams(collective_id=0, has_side_effects=True),
     )(rs, cs, ds)
@@ -351,12 +412,12 @@
         out_shape=[out, out],
         scratch_shapes=[pltpu.VMEM((512, 32 * ROWS), jnp.bfloat16), pltpu.VMEM((HALF, NB), jnp.float32)],
         compiler_params=pltpu.CompilerParams(vmem_limit_bytes=VMEM_LIMIT),
-    )(old_rank, new_rank, r_all.reshape(32, 2, 8, NB), c_all.reshape(32, 2, 8, NB), d_all, tu, tv, sk)
+    )(old_rank, new_rank, r_all.reshape(32, 2, 8, NB), c_all.reshape(32, 2, 8, NB), d_all.reshape(8, 4, ROWS, NB), tu, tv, sk)
 
 
 def on_device(diag_inverse, row_u, row_v, col_u, col_v, tile_u, tile_v, sketch, row_rank, col_rank, old_rank, new_rank):
     rs, cs, ds = prepare(row_rank, col_rank, diag_inverse, row_u[0].T, row_v[0].T, col_u[0].T, col_v[0].T)
-    r_all, c_all, d_all = gather(rs, cs, ds)
+    r_all, c_all, d_all = gather(rs, cs, ds.reshape(2, ROWS // 2, NB))
     new_u, new_v = update(old_rank, new_rank, r_all, c_all, d_all, tile_u[0, 0].T, tile_v[0, 0].T, sketch.T)
     return (new_u.T[None, None], new_v.T[None, None])
 

time: 92.7 us -> 75.2 us (0.81)
  the two profiles are of different devices: /device:TPU:39 before, /device:TPU:14 now
where the time goes in v2:
time: 75.2 us; the launch traced here: 73.8 us
  Pallas kernels  70.6 us (94%)
  between operations  3.22 us (4%)
    pallas_call x1, Pallas kernels, gather(): pl.pallas_call(gather_kernel, name='gather', in_specs=[anywhere] * 3, out...  54 us
    pallas_call x1, Pallas kernels, update(): pl.pallas_call(update_kernel, name='update', in_specs=[pl.BlockSpec(memor...  14.9 us
    pallas_call x1, Pallas kernels, prepare(): pl.pallas_call(prepare_kernel, name='prepare', in_specs=[pl.BlockSpec(mem...  1.67 us

profile of v2, /device:TPU:14, one launch (start us, length us, event | category | flops | bytes accessed | tf_op | source)
XLA Modules:
  0.0 73.8 jit_solution(2688816555327777103)
XLA Ops:
  3.2 1.7 %prepare.1 = (bf16[2,8,1376]{2,1,0:T(8,128)(2,1)}, bf16[2,8,1376]{2,1,0:T(8,128)(2,1)}, bf16[48,1376]{1,0:T(8,128)(2,1)}) custom-call(s32[1]{0:T(128)S(6)} %copy.14.row_rank, s32[1]{0:T(128)S(6)} %copy.15.col_rank, bf16[43,1376]{1,0:T(8,128)(2,1)} %diag.1, bf16[7,1376]{1,0:T(8,128)(2,1)} %bitcast.36, bf16[7,1376]{1,0:T(8,128)(2,1)} %bitcast.37, ...), custom_call_target="tpu_custom_call" | custom-call | tf_op jit(solution)/shard_map/prepare/pallas_call | solution.py:44
  4.9 54.0 %gather.1 = (bf16[8,4,2,8,1376]{4,3,2,1,0:T(8,128)(2,1)}, bf16[8,4,2,8,1376]{4,3,2,1,0:T(8,128)(2,1)}, bf16[8,4,2,24,1376]{4,3,2,1,0:T(8,128)(2,1)}) custom-call(bf16[2,8,1376]{2,1,0:T(8,128)(2,1)} %get-tuple-element.10.rs, bf16[2,8,1376]{2,1,0:T(8,128)(2,1)} %get-tuple-element.11.cs, bf16[2,24,1376]{2,1,0:T(8,128)(2,1)} %bitcast.35), custom_call_target="tpu_custom_call" | custom-call | tf_op jit(solution)/shard_map/gather/pallas_call | solution.py:305
  58.9 14.9 %update.1 = (bf16[224,1376]{1,0:T(8,128)(2,1)}, bf16[224,1376]{1,0:T(8,128)(2,1)}) custom-call(s32[1,1]{1,0:T(1,128)S(6)} %copy.16.old_rank, s32[1,1]{1,0:T(1,128)S(6)} %copy.17.new_rank, bf16[32,2,8,1376]{3,2,1,0:T(8,128)(2,1)} %bitcast.30, bf16[32,2,8,1376]{3,2,1,0:T(8,128)(2,1)} %bitcast.31, bf16[8,4,48,1376]{3,2,1,0:T(8,128)(2,1)} %bitcast.29, ...), custom_call_target="tpu_custom_call" | custom-call | tf_op jit(solution)/shard_map/update/pallas_call | solution.py:407

commit v3 on v2

--- a/solution.py
+++ b/solution.py
@@ -290,9 +290,8 @@
         if tick <= 4:
             x_tick(0, tick)
             z_tick(tick)
-        if tick >= 1:
             for t in (1, 3, 2):
-                x_tick(t, tick - 1)
+                x_tick(t, tick)
     for wait in ends:
         wait()
     for copy in local:

time: 75.2 us -> 78 us (1.037)
  the two profiles are of different devices: /device:TPU:14 before, /device:TPU:33 now
where the time goes in v3:
time: 78 us; the launch traced here: 77.8 us
  Pallas kernels  74.6 us (96%)
  between operations  3.22 us (4%)
    pallas_call x1, Pallas kernels, gather(): pl.pallas_call(gather_kernel, name='gather', in_specs=[anywhere] * 3, out...  58 us
    pallas_call x1, Pallas kernels, update(): pl.pallas_call(update_kernel, name='update', in_specs=[pl.BlockSpec(memor...  14.9 us
    pallas_call x1, Pallas kernels, prepare(): pl.pallas_call(prepare_kernel, name='prepare', in_specs=[pl.BlockSpec(mem...  1.67 us

profile of v3, /device:TPU:33, one launch (start us, length us, event | category | flops | bytes accessed | tf_op | source)
XLA Modules:
  0.0 77.8 jit_solution(10798314916051000369)
XLA Ops:
  3.2 1.7 %prepare.1 = (bf16[2,8,1376]{2,1,0:T(8,128)(2,1)}, bf16[2,8,1376]{2,1,0:T(8,128)(2,1)}, bf16[48,1376]{1,0:T(8,128)(2,1)}) custom-call(s32[1]{0:T(128)S(6)} %copy.14.row_rank, s32[1]{0:T(128)S(6)} %copy.15.col_rank, bf16[43,1376]{1,0:T(8,128)(2,1)} %diag.1, bf16[7,1376]{1,0:T(8,128)(2,1)} %bitcast.36, bf16[7,1376]{1,0:T(8,128)(2,1)} %bitcast.37, ...), custom_call_target="tpu_custom_call" | custom-call | tf_op jit(solution)/shard_map/prepare/pallas_call | solution.py:44
  4.9 58.0 %gather.1 = (bf16[8,4,2,8,1376]{4,3,2,1,0:T(8,128)(2,1)}, bf16[8,4,2,8,1376]{4,3,2,1,0:T(8,128)(2,1)}, bf16[8,4,2,24,1376]{4,3,2,1,0:T(8,128)(2,1)}) custom-call(bf16[2,8,1376]{2,1,0:T(8,128)(2,1)} %get-tuple-element.10.rs, bf16[2,8,1376]{2,1,0:T(8,128)(2,1)} %get-tuple-element.11.cs, bf16[2,24,1376]{2,1,0:T(8,128)(2,1)} %bitcast.35), custom_call_target="tpu_custom_call" | custom-call | tf_op jit(solution)/shard_map/gather/pallas_call | solution.py:304
  62.9 14.9 %update.1 = (bf16[224,1376]{1,0:T(8,128)(2,1)}, bf16[224,1376]{1,0:T(8,128)(2,1)}) custom-call(s32[1,1]{1,0:T(1,128)S(6)} %copy.16.old_rank, s32[1,1]{1,0:T(1,128)S(6)} %copy.17.new_rank, bf16[32,2,8,1376]{3,2,1,0:T(8,128)(2,1)} %bitcast.30, bf16[32,2,8,1376]{3,2,1,0:T(8,128)(2,1)} %bitcast.31, bf16[8,4,48,1376]{3,2,1,0:T(8,128)(2,1)} %bitcast.29, ...), custom_call_target="tpu_custom_call" | custom-call | tf_op jit(solution)/shard_map/update/pallas_call | solution.py:406
